TPU v7x, 32 devices: a whole 2x2x4 slice. The times are simulated.
32 devices in a mesh: sec: 4 (over y, core), row: 2 (over x), col: 4 (over z).
Axes of the slice: x: 2, y: 2, z: 4, core: 2. Of those that a mesh axis runs over, the one named last changes fastest.
Arguments:
- child_inv: bfloat16 [4, 4096, 4096], P('sec', 'col', 'row'), as said below
- child_low: bfloat16 [4, 2048, 4096], P('sec', 'row', 'col'), may hold values from -0.09375 to 0.09375
- parent_inv: bfloat16 [4, 6144, 3072], P('sec', 'col', 'row'), as said below
- parent_low: bfloat16 [4, 2048, 3072], P('sec', 'row', 'col'), may hold values from -0.078125 to 0.078125
- root_inv: bfloat16 [12288, 12288], P('col', ('sec', 'row')), as said below
- child_map: int32 [4, 2048], replicated, may hold values from 0 to 8191, as said below
- parent_map: int32 [2, 2048], replicated, may hold values from 0 to 12287, as said below
- child_rhs: float32 [4, 4096, 512], P('sec', 'row', 'col'), may hold values from -6 to 6
- parent_rhs: float32 [4, 3072, 512], P('sec', 'row', 'col'), may hold values from -6 to 6
- root_rhs: float32 [12288, 512], P(('sec', 'row'), 'col'), may hold values from -6 to 6
- child_back: float32 [4, 4096, 512], P('sec', 'col', 'row'), may hold values from -6 to 6
- parent_back: float32 [4, 3072, 512], P('sec', 'col', 'row'), may hold values from -6 to 6
- root_back: float32 [4, 3072, 512], P('col', ('sec', 'row')), may hold values from -6 to 6
Outputs:
- child_up: float32 [4, 4096, 512], P('sec', 'col', 'row')
- parent_up: float32 [4, 3072, 512], P('sec', 'col', 'row')
- root_up: float32 [4, 3072, 512], P('col', ('sec', 'row'))
- child_x: float32 [4, 4096, 512], P('sec', 'row', 'col')
- parent_x: float32 [4, 3072, 512], P('sec', 'row', 'col')
- root_x: float32 [12288, 512], P(('sec', 'row'), 'col')
Inputs may be any that keep to these rules, and one draw needn't show every extreme that they name: `child_inv`: zero above the diagonal of each child pivot block. `parent_inv`: the two halves side by side are zero above the diagonal. `root_inv`: zero above the diagonal. `child_map`: entries of one row are distinct; row s points into the front of parent s // 2. `parent_map`: entries of one row are distinct.
All inputs are finite; a program needn't handle non-finite values.
Results may differ from a plain program's by a relative error of at most 0.014.
Values may be sent and summed in bfloat16 or wider, within the bound.
No kernel may reach another device: no remote copies, remote signals or barrier semaphores. Data moves between devices by JAX's collectives and lax.ppermute only.
A program may use at most 128 MiB of HBM per device.

v0:
```python
import jax
import jax.numpy as jnp
from jax import lax
from jax.sharding import PartitionSpec as P

C1 = 2048
P2 = 6144
C2 = 2048
P3 = 12288


def from_partner(x, axis, bit):
    return lax.ppermute(x, axis, [(i, i ^ 1 << bit) for i in range(lax.axis_size(axis))])


def spread_cols(block):
    return lax.all_gather(block, "col", axis=1, tiled=True)


def spread_rows(block):
    return lax.all_gather(block, "row", axis=1, tiled=True)


def sum_rows(block):
    return lax.psum_scatter(block, "row", scatter_dimension=1, tiled=True)


def sum_cols(block):
    return lax.psum_scatter(block, "col", scatter_dimension=1, tiled=True)


def pair_sums(block):
    return from_partner(block, "sec", 0)


def pair_values(block):
    return from_partner(block, "sec", 0)


def root_gather(block):
    return lax.all_gather(block, ("sec", "row"), axis=0, tiled=True)


def matmul(left, right):
    return jnp.dot(left, right, preferred_element_type=jnp.float32)


def front_slot(target, n_row):
    pivot_rows = P2 // (2 * n_row)
    cont_rows = C2 // (2 * n_row)
    stride = pivot_rows + cont_rows
    half_size = P2 // 2
    pivot_slot = (
        target // half_size * n_row + target % half_size // pivot_rows
    ) * stride + target % pivot_rows
    offset = target - P2
    cont_slot = (
        (offset % (2 * cont_rows) // cont_rows * n_row + offset // (2 * cont_rows)) * stride
        + pivot_rows
        + offset % cont_rows
    )
    return jnp.where(target < P2, pivot_slot, cont_slot)


def place_rows(values, slots, first, count):
    local = slots - first
    inside = (local >= 0) & (local < count)
    target = jnp.where(inside, local, count)
    return jnp.zeros((count, values.shape[1]), jnp.float32).at[target].add(values, mode="drop")


def pair_reduce(block, pair_side):
    amount = block.shape[0] // 2
    keep = lax.dynamic_slice_in_dim(block, pair_side * amount, amount, 0)
    away = lax.dynamic_slice_in_dim(block, (1 - pair_side) * amount, amount, 0)
    return keep + pair_sums(away)


def pair_join(mine, other, pair_side):
    return jnp.where(
        pair_side == 0, jnp.concatenate([mine, other], 0), jnp.concatenate([other, mine], 0)
    )


def per_device(
    child_inv,
    child_low,
    parent_inv,
    parent_low,
    root_inv,
    child_map,
    parent_map,
    child_rhs,
    parent_rhs,
    root_rhs,
    child_back,
    parent_back,
    root_back,
):
    n_row = lax.axis_size("row")
    n_sec = lax.axis_size("sec")
    section = lax.axis_index("sec")
    row_id = lax.axis_index("row")
    pair_side = section % 2
    parent_id = section // 2
    place_id = section * n_row + row_id
    pivot_rows = P2 // (2 * n_row)
    cont_rows = C2 // (2 * n_row)
    stride = pivot_rows + cont_rows
    root_block = P3 // (n_sec * n_row)
    child_tile = child_inv[0]
    partial_value = matmul(child_tile, spread_cols(child_rhs[0].astype(jnp.bfloat16)))
    child_up = sum_rows(partial_value)
    solved = spread_rows(child_up.astype(jnp.bfloat16))
    contrib = -sum_cols(matmul(child_low[0], solved))
    own_map = lax.dynamic_slice_in_dim(child_map, section, 1, 0)[0]
    child_slots = front_slot(own_map, n_row)
    own_rows = lax.all_gather(contrib, "row", axis=0, tiled=True)
    partner_rows = pair_sums(own_rows)
    partner_map = lax.dynamic_slice_in_dim(child_map, section + 1 - 2 * pair_side, 1, 0)[0]
    first = (pair_side * n_row + row_id) * stride
    front = place_rows(own_rows, child_slots, first, stride) + place_rows(
        partner_rows, front_slot(partner_map, n_row), first, stride
    )
    pivot_in = parent_rhs[0] + front[:pivot_rows]
    share = sum_rows(matmul(parent_inv[0], spread_cols(pivot_in.astype(jnp.bfloat16))))
    parent_up = pair_reduce(share, pair_side)
    update = sum_cols(matmul(parent_low[0], spread_rows(parent_up.astype(jnp.bfloat16))))
    contrib_two = front[pivot_rows:] - pair_reduce(update, pair_side)
    map_row = lax.dynamic_slice_in_dim(parent_map, parent_id, 1, 0)[0]
    every = lax.all_gather(
        contrib_two.astype(jnp.bfloat16), ("sec", "row"), axis=0, tiled=True
    ).astype(contrib_two.dtype)
    order = parent_map.reshape(2, n_row, 2, cont_rows).transpose(0, 2, 1, 3).reshape(-1)
    root_front = place_rows(every, order, place_id * root_block, root_block)
    root_in = root_rhs + root_front
    root_wide = spread_cols(root_in.astype(jnp.bfloat16))
    root_part = matmul(root_inv, root_wide)
    root_up = lax.psum_scatter(
        root_part.astype(jnp.bfloat16), ("sec", "row"), scatter_dimension=0, tiled=True
    ).astype(jnp.float32)
    back_wide = root_gather(root_back[0].astype(jnp.bfloat16))
    root_x = sum_cols(matmul(root_inv.T, back_wide))
    root_all = root_gather(root_x.astype(jnp.bfloat16))
    block_targets = lax.dynamic_slice_in_dim(map_row, row_id * 2 * cont_rows, 2 * cont_rows)
    picked = jnp.take(root_all, block_targets, axis=0)
    residue = parent_back[0] - sum_rows(matmul(parent_low[0].T, spread_cols(picked)))
    residue_wide = spread_rows(residue.astype(jnp.bfloat16))
    full_residue = pair_join(residue_wide, pair_values(residue_wide), pair_side)
    parent_x = sum_cols(matmul(parent_inv[0].T, full_residue))
    own_cont = lax.dynamic_slice_in_dim(picked, pair_side * cont_rows, cont_rows, 0)
    front_x = jnp.concatenate([parent_x.astype(jnp.bfloat16), own_cont], 0)
    side_rows = lax.all_gather(front_x, "row", axis=0, tiled=True)
    whole_front = pair_join(side_rows, pair_values(side_rows), pair_side)
    child_count = C1 // n_row
    row_slots = lax.dynamic_slice_in_dim(child_slots, row_id * child_count, child_count)
    chosen = jnp.take(whole_front, row_slots, axis=0)
    residue_one = child_back[0] - sum_rows(matmul(child_low[0].T, spread_cols(chosen)))
    child_x = sum_cols(matmul(child_tile.T, spread_rows(residue_one.astype(jnp.bfloat16))))
    return (child_up[None], parent_up[None], root_up[None], child_x[None], parent_x[None], root_x)


def solution(mesh):
    return jax.shard_map(
        per_device,
        mesh=mesh,
        in_specs=(
            P("sec", "col", "row"),
            P("sec", "row", "col"),
            P("sec", "col", "row"),
            P("sec", "row", "col"),
            P("col", ("sec", "row")),
            P(),
            P(),
            P("sec", "row", "col"),
            P("sec", "row", "col"),
            P(("sec", "row"), "col"),
            P("sec", "col", "row"),
            P("sec", "col", "row"),
            P("col", ("sec", "row"), None),
        ),
        out_specs=(
            P("sec", "col", "row"),
            P("sec", "col", "row"),
            P("col", ("sec", "row"), None),
            P("sec", "row", "col"),
            P("sec", "row", "col"),
            P(("sec", "row"), "col"),
        ),
        check_vma=False,
    )
```

profile of v0, /device:TPU:0, one launch (start us, length us, event | category | flops | bytes accessed | tf_op | source)
XLA Modules:
  0.0 813.7 jit_solution(5113649186124741698)
XLA Ops:
  10.3 49.7 %all-gather.35.cloned.1.call-done = bf16[1,2048,512]{2,1,0:T(8,128)(2,1)} async-done(((bf16[1,2048,128]{2,1,0:T(8,128)(2,1)}), bf16[1,2048,512]{2,1,0:T(8,128)(2,1)}) %all-gather.35.cloned.1.call-update) | async-done | bytes 2097168 | tf_op jit(solution)/shard_map/all_gather | solution.py:17
  68.5 28.6 %reduce-scatter.13.cloned.1.call-done = f32[1024,256]{1,0:T(8,128)} async-done(((f32[1024,512]{1,0:T(8,128)}), f32[1024,256]{1,0:T(8,128)}) %reduce-scatter.13.cloned.1.call-update) | async-done | bytes 1048592 | tf_op jit(solution)/shard_map/reduce_scatter | solution.py:25
  99.3 17.9 %all-gather.37.cloned.1.call-done = bf16[1,3072,512]{2,1,0:T(8,128)(2,1)} async-done(((bf16[1,384,512]{2,1,0:T(8,128)(2,1)}), bf16[1,3072,512]{2,1,0:T(8,128)(2,1)}) %all-gather.37.cloned.1.call-update) | async-done | bytes 3145744 | tf_op jit(solution)/shard_map/all_gather | solution.py:41
  117.1 10.8 %fusion.18 = f32[1536,512]{1,0:T(8,128)} fusion(bf16[3072,1536]{1,0:T(8,128)(2,1)} %param.17, bf16[1,3072,512]{2,1,0:T(8,128)(2,1)} %all-gather.37.cloned.1.call-done), kind=kOutput, calls=%fused_computation.18 | convolution fusion | flops 4831838208 | bytes 15728640 | tf_op jit(solution)/shard_map/dot_general | solution.py:45
  128.0 12.3 %all-gather.15.cloned.1.call-done = bf16[1024,512]{1,0:T(8,128)(2,1)} async-done(((bf16[1024,256]{1,0:T(8,128)(2,1)}), bf16[1024,512]{1,0:T(8,128)(2,1)}) %all-gather.15.cloned.1.call-update) | async-done | bytes 1048592 | tf_op jit(solution)/shard_map/all_gather | solution.py:21
  144.2 44.3 %reduce-scatter.21.cloned.1.call-done = f32[1536,128]{1,0:T(8,128)} async-done(((f32[1536,512]{1,0:T(8,128)}), f32[1536,128]{1,0:T(8,128)}) %reduce-scatter.21.cloned.1.call-update) | async-done | bytes 786448 | tf_op jit(solution)/shard_map/reduce_scatter | solution.py:29
  190.5 43.7 %reduce-scatter.15.cloned.1.call-done = f32[1024,128]{0,1:T(8,128)} async-done(((f32[1024,512]{0,1:T(8,128)}), f32[1024,128]{0,1:T(8,128)}) %reduce-scatter.15.cloned.1.call-update) | async-done | bytes 524304 | tf_op jit(solution)/shard_map/reduce_scatter | solution.py:29
  243.2 13.4 %all-gather.17.cloned.1.call-done = f32[2048,128]{0,1:T(8,128)} async-done(((f32[1024,128]{0,1:T(8,128)}), f32[2048,128]{0,1:T(8,128)}) %all-gather.17.cloned.1.call-update) | async-done | bytes 1048592 | tf_op jit(solution)/shard_map/all_gather | solution.py:118
  260.9 12.3 %scatter_custom_fusion = f32[2048,128]{1,0:T(8,128)S(1)} fusion(s32[2048]{0:T(1024)S(1)} %bitcast.213, f32[2048,128]{1,0:T(8,128)} %copy.49, f32[]{:T(128)} %constant.180.clone.1), kind=kCustom, calls=%fused_computation.50 | custom fusion | flops 262144 | bytes 1049088 | tf_op jit(solution)/shard_map/scatter-add | solution.py:69
  277.0 12.1 %scatter_custom_fusion.1 = f32[2048,128]{1,0:T(8,128)S(1)} fusion(s32[2048]{0:T(1024)S(1)} %bitcast.212, f32[2048,128]{1,0:T(8,128)} %copy.50, f32[]{:T(128)} %constant.180.clone.1), kind=kCustom, calls=%fused_computation.48 | custom fusion | flops 262144 | bytes 1049088 | tf_op jit(solution)/shard_map/scatter-add | solution.py:69
  297.0 32.9 %all-gather.19.cloned.1.call-done = bf16[1536,512]{0,1:T(8,128)(2,1)} async-done(((bf16[1536,128]{0,1:T(8,128)(2,1)}), bf16[1536,512]{0,1:T(8,128)(2,1)}) %all-gather.19.cloned.1.call-update) | async-done | bytes 1572880 | tf_op jit(solution)/shard_map/all_gather | solution.py:17
  339.4 17.7 %reduce-scatter.23.cloned.1.call-done = f32[768,256]{0,1:T(8,128)} async-done(((f32[768,512]{0,1:T(8,128)}), f32[768,256]{0,1:T(8,128)}) %reduce-scatter.23.cloned.1.call-update) | async-done | bytes 786448 | tf_op jit(solution)/shard_map/reduce_scatter | solution.py:25
  358.6 15.3 %all_gather.52 = bf16[768,512]{0,1:T(8,128)(2,1)} all-gather(bf16[768,256]{0,1:T(8,128)(2,1)S(1)} %fusion.45), channel_id=1, replica_groups=mesh['sec'=4,'row'=2,'col'=4] {'row'}, dimensions={1}, use_global_device_ids=true | all-gather | bytes 1179648 | tf_op jit(solution)/shard_map/all_gather | solution.py:21
  384.2 21.1 %reduce-scatter.17.cloned.1.call-done = f32[1536,256]{0,1:T(8,128)} async-done(((f32[1536,512]{0,1:T(8,128)}), f32[1536,256]{0,1:T(8,128)}) %reduce-scatter.17.cloned.1.call-update) | async-done | bytes 1572880 | tf_op jit(solution)/shard_map/reduce_scatter | solution.py:25
  407.3 60.5 %reduce-scatter.25.cloned.1.call-done = f32[1536,128]{0,1:T(8,128)} async-done(((f32[1536,512]{0,1:T(8,128)}), f32[1536,128]{0,1:T(8,128)}) %reduce-scatter.25.cloned.1.call-update) | async-done | bytes 786448 | tf_op jit(solution)/shard_map/reduce_scatter | solution.py:29
  472.5 16.5 %all_gather.46 = bf16[768,512]{0,1:T(8,128)(2,1)S(1)} all-gather(bf16[768,256]{0,1:T(8,128)(2,1)S(1)} %get-tuple-element.32), channel_id=1, replica_groups=mesh['sec'=4,'row'=2,'col'=4] {'row'}, dimensions={1}, use_global_device_ids=true | all-gather | bytes 1179648 | tf_op jit(solution)/shard_map/all_gather | solution.py:21
  512.7 28.3 %reduce-scatter.19.cloned.1.call-done = f32[1024,128]{0,1:T(8,128)} async-done(((f32[1024,512]{0,1:T(8,128)}), f32[1024,128]{0,1:T(8,128)}) %reduce-scatter.19.cloned.1.call-update) | async-done | bytes 524304 | tf_op jit(solution)/shard_map/reduce_scatter | solution.py:29
  545.3 25.0 %all-gather.31.cloned.1.call-done = bf16[1024,512]{0,1:T(8,128)(2,1)} async-done(((bf16[1024,128]{0,1:T(8,128)(2,1)}), bf16[1024,512]{0,1:T(8,128)(2,1)}) %all-gather.31.cloned.1.call-update) | async-done | bytes 1048592 | tf_op jit(solution)/shard_map/all_gather | solution.py:17
  575.0 20.7 %all-gather.21.cloned.1.call-done = bf16[4096,128]{0,1:T(8,128)(2,1)} async-done(((bf16[512,128]{0,1:T(8,128)(2,1)}), bf16[4096,128]{0,1:T(8,128)(2,1)}) %all-gather.21.cloned.1.call-update) | async-done | bytes 1048592 | tf_op jit(solution)/shard_map/all_gather | solution.py:131
  597.2 22.7 %scatter_fusion = f32[1536,128]{1,0:T(8,128)S(1)} fusion(f32[1536,128]{1,0:T(8,128)S(1)} %copy-done.2, s32[4096]{0:T(1024)S(1)} %bitcast.205, f32[4096,128]{1,0:T(8,128)S(1)} %copy.54), kind=kCustom, calls=%fused_computation.4 | custom fusion | flops 524288 | bytes 6307840 | tf_op jit(solution)/shard_map/scatter-add | solution.py:69
  632.1 37.5 %all-gather.23.cloned.1.call-done = bf16[1536,512]{1,0:T(8,128)(2,1)} async-done(((bf16[1536,128]{1,0:T(8,128)(2,1)}), bf16[1536,512]{1,0:T(8,128)(2,1)}) %all-gather.23.cloned.1.call-update) | async-done | bytes 1572880 | tf_op jit(solution)/shard_map/all_gather | solution.py:17
  680.7 10.6 %all-gather.33.cloned.1.call-done = bf16[1024,512]{0,1:T(8,128)(2,1)} async-done(((bf16[1024,256]{0,1:T(8,128)(2,1)}), bf16[1024,512]{0,1:T(8,128)(2,1)}) %all-gather.33.cloned.1.call-update) | async-done | bytes 1048592 | tf_op jit(solution)/shard_map/all_gather | solution.py:21
  701.6 23.3 %reduce-scatter.31.cloned.1.call-done = bf16[384,512]{1,0:T(8,128)(2,1)} async-done(((bf16[3072,512]{1,0:T(8,128)(2,1)}), bf16[384,512]{1,0:T(8,128)(2,1)}) %reduce-scatter.31.cloned.1.call-update) | async-done | bytes 393232
  727.3 76.5 %reduce-scatter.29.cloned.1.call-done = f32[2048,128]{0,1:T(8,128)} async-done(((f32[2048,512]{0,1:T(8,128)}), f32[2048,128]{0,1:T(8,128)}) %reduce-scatter.29.cloned.1.call-update) | async-done | bytes 1048592 | tf_op jit(solution)/shard_map/reduce_scatter | solution.py:29
  (153 shorter events, 144.1 us)
Async XLA Ops:
  8.0 52.0 %all-gather.35.cloned.1.call-start = ((), (), s32[]{:S(2)}) async-start(), calls=%async_computation.29 | async-start | bytes 2621440 | tf_op jit(solution)/shard_map/all_gather | solution.py:17
  10.3 86.9 %reduce-scatter.13.cloned.1.call-start = ((), (), s32[]{:S(2)}) async-start(), calls=%async_computation.10 | async-start | bytes 3145728 | tf_op jit(solution)/shard_map/reduce_scatter | solution.py:25
  66.5 50.6 %all-gather.37.cloned.1.call-start = ((), (), s32[]{:S(2)}) async-start(), calls=%async_computation.30 | async-start | bytes 3538944 | tf_op jit(solution)/shard_map/all_gather | solution.py:41
  68.5 71.8 %all-gather.15.cloned.1.call-start = ((), (), s32[]{:S(2)}) async-start(), calls=%async_computation.11 | async-start | bytes 1572864 | tf_op jit(solution)/shard_map/all_gather | solution.py:21
  99.2 89.3 %reduce-scatter.21.cloned.1.call-start = ((), (), s32[]{:S(2)}) async-start(), calls=%async_computation.19 | async-start | bytes 3932160 | tf_op jit(solution)/shard_map/reduce_scatter | solution.py:29
  127.9 106.3 %reduce-scatter.15.cloned.1.call-start = ((), (), s32[]{:S(2)}) async-start(), calls=%async_computation.12 | async-start | bytes 2621440 | tf_op jit(solution)/shard_map/reduce_scatter | solution.py:29
  144.2 92.9 %all-gather.25.cloned.1.call-start = ((), (), s32[]{:S(2)}) async-start(), calls=%async_computation.20 | async-start | bytes 3538944 | tf_op jit(solution)/shard_map/all_gather | solution.py:41
  190.4 66.2 %all-gather.17.cloned.1.call-start = ((), (), s32[]{:S(2)}) async-start(), calls=%async_computation.13 | async-start | bytes 1572864 | tf_op jit(solution)/shard_map/all_gather | solution.py:118
  236.1 57.0 %all-gather.27.cloned.1.call-start = ((), (), s32[]{:S(2)}) async-start(), calls=%async_computation.21 | async-start | bytes 1310720 | tf_op jit(solution)/shard_map/all_gather | solution.py:17
  243.1 86.8 %all-gather.19.cloned.1.call-start = ((), (), s32[]{:S(2)}) async-start(), calls=%async_computation.14 | async-start | bytes 1966080 | tf_op jit(solution)/shard_map/all_gather | solution.py:17
  256.6 17.8 %collective-permute-start = (f32[2048,128]{0,1:T(8,128)}, f32[2048,128]{0,1:T(8,128)}, u32[]{:S(2)}, u32[]{:S(2)}) collective-permute-start(f32[2048,128]{0,1:T(8,128)} %all-gather.17.cloned.1.call-done), channel_id=1, source_target_pairs={{0,8},{8,0},{16,24},{24,16},{1,9},{9,1},{17,25},{25,17},{2,10},{10... | collective-permute-start | bytes 3145736 | tf_op jit(solution)/shard_map/ppermute | solution.py:13
  293.0 64.1 %reduce-scatter.23.cloned.1.call-start = ((), (), s32[]{:S(2)}) async-start(), calls=%async_computation.22 | async-start | bytes 2359296 | tf_op jit(solution)/shard_map/reduce_scatter | solution.py:25
  297.0 108.3 %reduce-scatter.17.cloned.1.call-start = ((), (), s32[]{:S(2)}) async-start(), calls=%async_computation.15 | async-start | bytes 4718592 | tf_op jit(solution)/shard_map/reduce_scatter | solution.py:25
  337.1 130.8 %reduce-scatter.25.cloned.1.call-start = ((), (), s32[]{:S(2)}) async-start(), calls=%async_computation.23 | async-start | bytes 3932160 | tf_op jit(solution)/shard_map/reduce_scatter | solution.py:29
  384.1 110.8 %all-gather.29.cloned.1.call-start = ((), (), s32[]{:S(2)}) async-start(), calls=%async_computation.24 | async-start | bytes 1572864 | tf_op jit(solution)/shard_map/all_gather | solution.py:153
  407.3 62.7 %collective-permute-start.1 = (f32[768,256]{0,1:T(8,128)}, f32[768,256]{0,1:T(8,128)}, u32[]{:S(2)}, u32[]{:S(2)}) collective-permute-start(f32[768,256]{0,1:T(8,128)} %constant_dynamic-slice_fusion.2), channel_id=1, source_target_pairs={{0,8},{8,0},{16,24},{24,16},{1,9},{9,1},{17,25},{25,17},{2,10},{10... | collective-permute-start | bytes 2359304 | tf_op jit(solution)/shard_map/ppermute | solution.py:13
  469.9 71.1 %reduce-scatter.19.cloned.1.call-start = ((), (), s32[]{:S(2)}) async-start(), calls=%async_computation.16 | async-start | bytes 2621440 | tf_op jit(solution)/shard_map/reduce_scatter | solution.py:29
  491.3 79.0 %all-gather.31.cloned.1.call-start = ((), (), s32[]{:S(2)}) async-start(), calls=%async_computation.25 | async-start | bytes 1310720 | tf_op jit(solution)/shard_map/all_gather | solution.py:17
  512.6 83.0 %all-gather.21.cloned.1.call-start = ((), (), s32[]{:S(2)}) async-start(), calls=%async_computation.17 | async-start | bytes 1179648 | tf_op jit(solution)/shard_map/all_gather | solution.py:131
  545.3 84.6 %reduce-scatter.27.cloned.1.call-start = ((), (), s32[]{:S(2)}) async-start(), calls=%async_computation.26 | async-start | bytes 3145728 | tf_op jit(solution)/shard_map/reduce_scatter | solution.py:25
  574.2 95.4 %all-gather.23.cloned.1.call-start = ((), (), s32[]{:S(2)}) async-start(), calls=%async_computation.18 | async-start | bytes 1966080 | tf_op jit(solution)/shard_map/all_gather | solution.py:17
  620.7 70.6 %all-gather.33.cloned.1.call-start = ((), (), s32[]{:S(2)}) async-start(), calls=%async_computation.27 | async-start | bytes 1572864 | tf_op jit(solution)/shard_map/all_gather | solution.py:21
  632.0 92.8 %reduce-scatter.31.cloned.1.call-start = ((), (), s32[]{:S(2)}) async-start(), calls=%async_computation.31 | async-start | bytes 3538944
  680.6 123.2 %reduce-scatter.29.cloned.1.call-start = ((), (), s32[]{:S(2)}) async-start(), calls=%async_computation.28 | async-start | bytes 5242880 | tf_op jit(solution)/shard_map/reduce_scatter | solution.py:29
  (18 other events, 323.1 us)
Sparse Core Ops, SparseCore 0:
  11.0 48.9 all-gather.34
  66.7 30.4 reduce-scatter.12
  128.1 60.3 reduce-scatter.20
  190.6 43.5 reduce-scatter.14
  470.0 24.8 all-gather.28
  497.1 43.8 reduce-scatter.18
  543.1 27.1 all-gather.30
  572.8 22.8 all-gather.20
  597.9 31.8 reduce-scatter.26
  631.9 37.6 all-gather.22
  671.7 19.4 all-gather.32
Sparse Core Ops, SparseCore 1:
  69.5 47.6 all-gather.36
  119.1 21.1 all-gather.14
  190.5 31.9 all-gather.24
  236.2 20.4 all-gather.16
  258.8 27.9 all-gather.26
  293.1 36.8 all-gather.18
  332.1 25.0 reduce-scatter.22
  359.2 46.0 reduce-scatter.16
  407.4 60.4 reduce-scatter.24
  680.7 44.1 reduce-scatter.30
  727.0 76.7 reduce-scatter.28
where the time goes:
time: 815 us; the launch traced here: 814 us
  waiting for transfers between devices  583 us (72%)
  other arithmetic  75.1 us (9%)
  matrix products  61 us (7%)
  local copies, waits for them, and re-layouts  45.6 us (6%)
  blocking collectives  31.8 us (4%)
  between operations  16.1 us (2%)
    reduce_scatter x5, waiting for transfers between devices, sum_cols(): return lax.psum_scatter(block, 'col', scatter_dimension=1, tiled=True)  253 us
    all_gather x5, waiting for transfers between devices, spread_cols(): return lax.all_gather(block, 'col', axis=1, tiled=True)  145 us
    reduce_scatter x4, waiting for transfers between devices, sum_rows(): return lax.psum_scatter(block, 'row', scatter_dimension=1, tiled=True)  75.6 us
    dot_general x10, matrix products, matmul(): return jnp.dot(left, right, preferred_element_type=jnp.float32)  61 us
    scatter-add x3, other arithmetic, place_rows(): jnp.zeros((count, values.shape[1]), jnp.float32).at[target]  47 us
    all_gather x2, blocking collectives, spread_rows(): return lax.all_gather(block, 'row', axis=1, tiled=True)  31.8 us
    unnamed x23, waiting for transfers between devices  23.6 us
    all_gather x2, waiting for transfers between devices, spread_rows(): return lax.all_gather(block, 'row', axis=1, tiled=True)  22.8 us
  transfers between devices with their start and end apart: 27, of which 23 were waited for; matrix products, arithmetic and copies ran while one was open for 21% of the time, Pallas kernels for 0%

commit v1 on v0

--- a/solution.py
+++ b/solution.py
@@ -18,7 +18,9 @@
 
 
 def spread_rows(block):
-    return lax.all_gather(block, "row", axis=1, tiled=True)
+    return jnp.concatenate(
+        lax.all_to_all(jnp.stack([block] * lax.axis_size("row")), "row", 0, 0), axis=1
+    )
 
 
 def sum_rows(block):

time: 815 us -> 842 us (1.033)
  blocking collectives: 31.8 us -> 66.7 us
  waiting for transfers between devices: 583 us -> 572 us
    all_to_all x0 -> x4, blocking collectives: none -> 66.7 us  [spread_rows(): lax.all_to_all(jnp.stack([block] * lax.axis_size('row')), 'row', 0, 0)]
    all_gather x2, waiting for transfers between devices: 17.9 us -> 57.1 us  [root_gather(): return lax.all_gather(block, ('sec', 'row'), axis=0, tiled=True)]
    all_gather x2 -> x0, blocking collectives: 31.8 us -> none  [spread_rows(): return lax.all_gather(block, 'row', axis=1, tiled=True)]
    all_gather x5, waiting for transfers between devices: 145 us -> 119 us  [spread_cols(): return lax.all_gather(block, 'col', axis=1, tiled=True)]
    all_gather x2 -> x0, waiting for transfers between devices: 22.8 us -> none  [spread_rows(): return lax.all_gather(block, 'row', axis=1, tiled=True)]
    all_gather x1, waiting for transfers between devices: 3.57 us -> 19.2 us  [per_device(): side_rows = lax.all_gather(front_x, 'row', axis=0, tiled=True)]
    all_gather x1, waiting for transfers between devices: 20.7 us -> 8.81 us  [per_device(): lax.all_gather(contrib_two.astype(jnp.bfloat16), ('sec', 'row'), axis=0,...]
    reduce_scatter x5, waiting for transfers between devices: 253 us -> 243 us  [sum_cols(): return lax.psum_scatter(block, 'col', scatter_dimension=1, tiled=True)]
  transfers between devices with their start and end apart: 27 -> 25, of which waited for: 23 -> 22; matrix products, arithmetic and copies ran while one was open for 21% -> 22% of each run, Pallas kernels for 0% -> 0%
where the time goes in v1:
time: 842 us; the launch traced here: 840 us
  waiting for transfers between devices  572 us (68%)
  other arithmetic  76.6 us (9%)
  blocking collectives  66.7 us (8%)
  matrix products  59.8 us (7%)
  local copies, waits for them, and re-layouts  50 us (6%)
  between operations  14.7 us (2%)
    reduce_scatter x5, waiting for transfers between devices, sum_cols(): return lax.psum_scatter(block, 'col', scatter_dimension=1, tiled=True)  243 us
    all_gather x5, waiting for transfers between devices, spread_cols(): return lax.all_gather(block, 'col', axis=1, tiled=True)  119 us
    reduce_scatter x4, waiting for transfers between devices, sum_rows(): return lax.psum_scatter(block, 'row', scatter_dimension=1, tiled=True)  76.7 us
    all_to_all x4, blocking collectives, spread_rows(): lax.all_to_all(jnp.stack([block] * lax.axis_size('row')), 'row', 0, 0)  66.7 us
    dot_general x10, matrix products, matmul(): return jnp.dot(left, right, preferred_element_type=jnp.float32)  59.8 us
    all_gather x2, waiting for transfers between devices, root_gather(): return lax.all_gather(block, ('sec', 'row'), axis=0, tiled=True)  57.1 us
    scatter-add x3, other arithmetic, place_rows(): jnp.zeros((count, values.shape[1]), jnp.float32).at[target]  47.5 us
    unnamed x21, waiting for transfers between devices  24.1 us
  transfers between devices with their start and end apart: 25, of which 22 were waited for; matrix products, arithmetic and copies ran while one was open for 22% of the time, Pallas kernels for 0%

profile of v1, /device:TPU:0, one launch (start us, length us, event | category | flops | bytes accessed | tf_op | source)
XLA Modules:
  0.0 840.5 jit_solution(15535686813954171231)
XLA Ops:
  11.5 47.7 %all-gather.29.cloned.1.call-done = bf16[1,2048,512]{2,1,0:T(8,128)(2,1)} async-done(((bf16[1,2048,128]{2,1,0:T(8,128)(2,1)}), bf16[1,2048,512]{2,1,0:T(8,128)(2,1)}) %all-gather.29.cloned.1.call-update) | async-done | bytes 2097168 | tf_op jit(solution)/shard_map/all_gather | solution.py:17
  65.8 26.2 %all-gather.31.cloned.1.call-done = bf16[1,3072,512]{2,1,0:T(8,128)(2,1)} async-done(((bf16[1,384,512]{2,1,0:T(8,128)(2,1)}), bf16[1,3072,512]{2,1,0:T(8,128)(2,1)}) %all-gather.31.cloned.1.call-update) | async-done | bytes 3145744 | tf_op jit(solution)/shard_map/all_gather | solution.py:43
  102.8 23.9 %reduce-scatter.13.cloned.1.call-done = f32[1024,256]{1,0:T(8,128)} async-done(((f32[1024,512]{1,0:T(8,128)}), f32[1024,256]{1,0:T(8,128)}) %reduce-scatter.13.cloned.1.call-update) | async-done | bytes 1048592 | tf_op jit(solution)/shard_map/reduce_scatter | solution.py:27
  128.1 16.1 %all_to_all.20 = bf16[2,1024,256]{2,1,0:T(8,128)(2,1)S(1)} all-to-all(bf16[2,1024,256]{2,1,0:T(8,128)(2,1)S(1)} %pad_maximum_fusion), channel_id=1, replica_groups=mesh['sec'=4,'row'=2,'col'=4] {'row'}, dimensions={0} | all-to-all | bytes 2097152 | tf_op jit(solution)/shard_map/all_to_all | solution.py:22
  149.5 40.4 %reduce-scatter.21.cloned.1.call-done = f32[1536,128]{1,0:T(8,128)} async-done(((f32[1536,512]{1,0:T(8,128)}), f32[1536,128]{1,0:T(8,128)}) %reduce-scatter.21.cloned.1.call-update) | async-done | bytes 786448 | tf_op jit(solution)/shard_map/reduce_scatter | solution.py:31
  191.9 43.7 %reduce-scatter.15.cloned.1.call-done = f32[1024,128]{0,1:T(8,128)} async-done(((f32[1024,512]{0,1:T(8,128)}), f32[1024,128]{0,1:T(8,128)}) %reduce-scatter.15.cloned.1.call-update) | async-done | bytes 524304 | tf_op jit(solution)/shard_map/reduce_scatter | solution.py:31
  238.4 30.9 %all-gather.21.cloned.1.call-done = bf16[12288,128]{1,0:T(8,128)(2,1)} async-done(((bf16[1536,128]{1,0:T(8,128)(2,1)}), bf16[12288,128]{1,0:T(8,128)(2,1)}) %all-gather.21.cloned.1.call-update) | async-done | bytes 3145744 | tf_op jit(solution)/shard_map/all_gather | solution.py:43
  275.5 17.3 %all-gather.13.cloned.1.call-done = f32[2048,128]{0,1:T(8,128)} async-done(((f32[1024,128]{0,1:T(8,128)}), f32[2048,128]{0,1:T(8,128)}) %all-gather.13.cloned.1.call-update) | async-done | bytes 1048592 | tf_op jit(solution)/shard_map/all_gather | solution.py:120
  297.0 12.3 %scatter_custom_fusion = f32[2048,128]{1,0:T(8,128)S(1)} fusion(s32[2048]{0:T(1024)S(1)} %bitcast.240, f32[2048,128]{1,0:T(8,128)} %copy.53, f32[]{:T(128)} %constant.180.clone.1), kind=kCustom, calls=%fused_computation.56 | custom fusion | flops 262144 | bytes 1049088 | tf_op jit(solution)/shard_map/scatter-add | solution.py:71
  313.2 12.1 %scatter_custom_fusion.1 = f32[2048,128]{1,0:T(8,128)S(1)} fusion(s32[2048]{0:T(1024)S(1)} %bitcast.239, f32[2048,128]{1,0:T(8,128)} %copy.54, f32[]{:T(128)} %constant.180.clone.1), kind=kCustom, calls=%fused_computation.54 | custom fusion | flops 262144 | bytes 1049088 | tf_op jit(solution)/shard_map/scatter-add | solution.py:71
  333.2 33.2 %all-gather.15.cloned.1.call-done = bf16[1536,512]{0,1:T(8,128)(2,1)} async-done(((bf16[1536,128]{0,1:T(8,128)(2,1)}), bf16[1536,512]{0,1:T(8,128)(2,1)}) %all-gather.15.cloned.1.call-update) | async-done | bytes 1572880 | tf_op jit(solution)/shard_map/all_gather | solution.py:17
  375.9 17.7 %reduce-scatter.23.cloned.1.call-done = f32[768,256]{0,1:T(8,128)} async-done(((f32[768,512]{0,1:T(8,128)}), f32[768,256]{0,1:T(8,128)}) %reduce-scatter.23.cloned.1.call-update) | async-done | bytes 786448 | tf_op jit(solution)/shard_map/reduce_scatter | solution.py:27
  395.1 20.6 %all_to_all.21 = bf16[2,768,256]{1,2,0:T(8,128)(2,1)} all-to-all(bf16[2,768,256]{1,2,0:T(8,128)(2,1)S(1)} %pad_maximum_fusion.3), channel_id=1, replica_groups=mesh['sec'=4,'row'=2,'col'=4] {'row'}, dimensions={0} | all-to-all | bytes 1572864 | tf_op jit(solution)/shard_map/all_to_all | solution.py:22
  426.2 18.4 %reduce-scatter.17.cloned.1.call-done = f32[1536,256]{0,1:T(8,128)} async-done(((f32[1536,512]{0,1:T(8,128)}), f32[1536,256]{0,1:T(8,128)}) %reduce-scatter.17.cloned.1.call-update) | async-done | bytes 1572880 | tf_op jit(solution)/shard_map/reduce_scatter | solution.py:27
  451.7 13.8 %all_to_all.22 = bf16[2,768,256]{1,2,0:T(8,128)(2,1)S(1)} all-to-all(bf16[2,768,256]{1,2,0:T(8,128)(2,1)S(1)} %pad_maximum_fusion.2), channel_id=1, replica_groups=mesh['sec'=4,'row'=2,'col'=4] {'row'}, dimensions={0} | all-to-all | bytes 1572864 | tf_op jit(solution)/shard_map/all_to_all | solution.py:22
  468.8 38.4 %reduce-scatter.25.cloned.1.call-done = f32[1536,128]{0,1:T(8,128)} async-done(((f32[1536,512]{0,1:T(8,128)}), f32[1536,128]{0,1:T(8,128)}) %reduce-scatter.25.cloned.1.call-update) | async-done | bytes 786448 | tf_op jit(solution)/shard_map/reduce_scatter | solution.py:31
  509.3 43.7 %reduce-scatter.19.cloned.1.call-done = f32[1024,128]{0,1:T(8,128)} async-done(((f32[1024,512]{0,1:T(8,128)}), f32[1024,128]{0,1:T(8,128)}) %reduce-scatter.19.cloned.1.call-update) | async-done | bytes 524304 | tf_op jit(solution)/shard_map/reduce_scatter | solution.py:31
  556.3 19.2 %all-gather.25.cloned.1.call-done = bf16[4096,128]{0,1:T(8,128)(2,1)} async-done(((bf16[2048,128]{0,1:T(8,128)(2,1)}), bf16[4096,128]{0,1:T(8,128)(2,1)}) %all-gather.25.cloned.1.call-update) | async-done | bytes 1048592 | tf_op jit(solution)/shard_map/all_gather | solution.py:155
  603.9 23.2 %scatter_fusion = f32[1536,128]{1,0:T(8,128)S(1)} fusion(f32[1536,128]{1,0:T(8,128)S(1)} %copy-done.1, s32[4096]{0:T(1024)S(1)} %bitcast.232, f32[4096,128]{1,0:T(8,128)} %copy.58), kind=kCustom, calls=%fused_computation.4 | custom fusion | flops 524288 | bytes 6307840 | tf_op jit(solution)/shard_map/scatter-add | solution.py:71
  635.3 35.1 %all-gather.19.cloned.1.call-done = bf16[1536,512]{1,0:T(8,128)(2,1)} async-done(((bf16[1536,128]{1,0:T(8,128)(2,1)}), bf16[1536,512]{1,0:T(8,128)(2,1)}) %all-gather.19.cloned.1.call-update) | async-done | bytes 1572880 | tf_op jit(solution)/shard_map/all_gather | solution.py:17
  686.1 16.6 %reduce-scatter.27.cloned.1.call-done = f32[1024,256]{0,1:T(8,128)} async-done(((f32[1024,512]{0,1:T(8,128)}), f32[1024,256]{0,1:T(8,128)}) %reduce-scatter.27.cloned.1.call-update) | async-done | bytes 1048592 | tf_op jit(solution)/shard_map/reduce_scatter | solution.py:27
  704.3 16.2 %all_to_all.23 = bf16[2,1024,256]{1,2,0:T(8,128)(2,1)S(1)} all-to-all(bf16[2,1024,256]{1,2,0:T(8,128)(2,1)S(1)} %pad_maximum_fusion.1), channel_id=1, replica_groups=mesh['sec'=4,'row'=2,'col'=4] {'row'}, dimensions={0} | all-to-all | bytes 2097152 | tf_op jit(solution)/shard_map/all_to_all | solution.py:22
  728.3 23.8 %reduce-scatter.31.cloned.1.call-done = bf16[384,512]{1,0:T(8,128)(2,1)} async-done(((bf16[3072,512]{1,0:T(8,128)(2,1)}), bf16[384,512]{1,0:T(8,128)(2,1)}) %reduce-scatter.31.cloned.1.call-update) | async-done | bytes 393232
  754.6 76.5 %reduce-scatter.29.cloned.1.call-done = f32[2048,128]{0,1:T(8,128)} async-done(((f32[2048,512]{0,1:T(8,128)}), f32[2048,128]{0,1:T(8,128)}) %reduce-scatter.29.cloned.1.call-update) | async-done | bytes 1048592 | tf_op jit(solution)/shard_map/reduce_scatter | solution.py:31
  (146 shorter events, 158.6 us)
Async XLA Ops:
  7.2 52.0 %all-gather.29.cloned.1.call-start = ((), (), s32[]{:S(2)}) async-start(), calls=%async_computation.31 | async-start | bytes 2621440 | tf_op jit(solution)/shard_map/all_gather | solution.py:17
  9.4 82.6 %all-gather.31.cloned.1.call-start = ((), (), s32[]{:S(2)}) async-start(), calls=%async_computation.32 | async-start | bytes 3538944 | tf_op jit(solution)/shard_map/all_gather | solution.py:43
  11.4 115.3 %reduce-scatter.13.cloned.1.call-start = ((), (), s32[]{:S(2)}) async-start(), calls=%async_computation.14 | async-start | bytes 3145728 | tf_op jit(solution)/shard_map/reduce_scatter | solution.py:27
  65.8 124.2 %reduce-scatter.21.cloned.1.call-start = ((), (), s32[]{:S(2)}) async-start(), calls=%async_computation.22 | async-start | bytes 3932160 | tf_op jit(solution)/shard_map/reduce_scatter | solution.py:31
  102.8 132.8 %reduce-scatter.15.cloned.1.call-start = ((), (), s32[]{:S(2)}) async-start(), calls=%async_computation.15 | async-start | bytes 2621440 | tf_op jit(solution)/shard_map/reduce_scatter | solution.py:31
  149.5 119.9 %all-gather.21.cloned.1.call-start = ((), (), s32[]{:S(2)}) async-start(), calls=%async_computation.23 | async-start | bytes 3538944 | tf_op jit(solution)/shard_map/all_gather | solution.py:43
  191.9 100.9 %all-gather.13.cloned.1.call-start = ((), (), s32[]{:S(2)}) async-start(), calls=%async_computation.16 | async-start | bytes 1572864 | tf_op jit(solution)/shard_map/all_gather | solution.py:120
  237.5 91.7 %all-gather.23.cloned.1.call-start = ((), (), s32[]{:S(2)}) async-start(), calls=%async_computation.24 | async-start | bytes 1310720 | tf_op jit(solution)/shard_map/all_gather | solution.py:17
  275.4 91.0 %all-gather.15.cloned.1.call-start = ((), (), s32[]{:S(2)}) async-start(), calls=%async_computation.17 | async-start | bytes 1966080 | tf_op jit(solution)/shard_map/all_gather | solution.py:17
  292.8 17.8 %collective-permute-start = (f32[2048,128]{0,1:T(8,128)}, f32[2048,128]{0,1:T(8,128)}, u32[]{:S(2)}, u32[]{:S(2)}) collective-permute-start(f32[2048,128]{0,1:T(8,128)} %all-gather.13.cloned.1.call-done), channel_id=1, source_target_pairs={{0,8},{8,0},{16,24},{24,16},{1,9},{9,1},{17,25},{25,17},{2,10},{10... | collective-permute-start | bytes 3145736 | tf_op jit(solution)/shard_map/ppermute | solution.py:13
  329.2 64.4 %reduce-scatter.23.cloned.1.call-start = ((), (), s32[]{:S(2)}) async-start(), calls=%async_computation.25 | async-start | bytes 2359296 | tf_op jit(solution)/shard_map/reduce_scatter | solution.py:27
  333.1 111.4 %reduce-scatter.17.cloned.1.call-start = ((), (), s32[]{:S(2)}) async-start(), calls=%async_computation.18 | async-start | bytes 4718592 | tf_op jit(solution)/shard_map/reduce_scatter | solution.py:27
  373.5 133.6 %reduce-scatter.25.cloned.1.call-start = ((), (), s32[]{:S(2)}) async-start(), calls=%async_computation.26 | async-start | bytes 3932160 | tf_op jit(solution)/shard_map/reduce_scatter | solution.py:31
  415.7 2.6 collective-permute-start.3
  426.1 126.9 %reduce-scatter.19.cloned.1.call-start = ((), (), s32[]{:S(2)}) async-start(), calls=%async_computation.19 | async-start | bytes 2621440 | tf_op jit(solution)/shard_map/reduce_scatter | solution.py:31
  467.9 107.6 %all-gather.25.cloned.1.call-start = ((), (), s32[]{:S(2)}) async-start(), calls=%async_computation.27 | async-start | bytes 1572864 | tf_op jit(solution)/shard_map/all_gather | solution.py:155
  509.2 92.1 %all-gather.17.cloned.1.call-start = ((), (), s32[]{:S(2)}) async-start(), calls=%async_computation.20 | async-start | bytes 1179648 | tf_op jit(solution)/shard_map/all_gather | solution.py:133
  554.7 20.8 %collective-permute-start.2 = (f32[512,128]{0,1:T(8,128)}, f32[512,128]{0,1:T(8,128)S(1)}, u32[]{:S(2)}, u32[]{:S(2)}) collective-permute-start(f32[512,128]{0,1:T(8,128)} %constant_dynamic-slice_fusion.1), channel_id=1, source_target_pairs={{0,8},{8,0},{16,24},{24,16},{1,9},{9,1},{17,25},{25,17},{2,10},{10... | collective-permute-start | bytes 786440 | tf_op jit(solution)/shard_map/ppermute | solution.py:13
  575.5 3.0 collective-permute-start.4
  577.2 54.1 %all-gather.27.cloned.1.call-start = ((), (), s32[]{:S(2)}) async-start(), calls=%async_computation.28 | async-start | bytes 1310720 | tf_op jit(solution)/shard_map/all_gather | solution.py:17
  592.3 78.1 %all-gather.19.cloned.1.call-start = ((), (), s32[]{:S(2)}) async-start(), calls=%async_computation.21 | async-start | bytes 1966080 | tf_op jit(solution)/shard_map/all_gather | solution.py:17
  627.9 74.7 %reduce-scatter.27.cloned.1.call-start = ((), (), s32[]{:S(2)}) async-start(), calls=%async_computation.29 | async-start | bytes 3145728 | tf_op jit(solution)/shard_map/reduce_scatter | solution.py:27
  635.2 116.9 %reduce-scatter.31.cloned.1.call-start = ((), (), s32[]{:S(2)}) async-start(), calls=%async_computation.33 | async-start | bytes 3538944
  684.4 146.7 %reduce-scatter.29.cloned.1.call-start = ((), (), s32[]{:S(2)}) async-start(), calls=%async_computation.30 | async-start | bytes 5242880 | tf_op jit(solution)/shard_map/reduce_scatter | solution.py:31
  (12 other events, 261.9 us)
Sparse Core Ops, SparseCore 0:
  10.1 48.9 all-gather.28
  61.6 30.3 all-gather.30
  94.8 31.8 reduce-scatter.12
  129.5 60.3 reduce-scatter.20
  192.1 43.5 reduce-scatter.14
  237.9 31.3 all-gather.20
  271.5 21.2 all-gather.12
  294.9 27.9 all-gather.22
  329.3 37.0 all-gather.14
  368.5 25.0 reduce-scatter.22
  395.8 48.6 reduce-scatter.16
  446.7 60.4 reduce-scatter.24
  509.5 43.5 reduce-scatter.18
  555.0 20.4 all-gather.24
  577.8 23.4 all-gather.16
  603.3 27.9 all-gather.26
  633.3 37.0 all-gather.18
  672.5 30.1 reduce-scatter.26
  706.1 46.0 reduce-scatter.30
  754.3 76.7 reduce-scatter.28
